TPU v7x, 32 devices: a whole 2x2x4 slice. The times are simulated.
32 devices in a mesh: dom: 8 (over z, x), group: 4 (over y, core).
Axes of the slice: x: 2, y: 2, z: 4, core: 2. Of those that a mesh axis runs over, the one named last changes fastest.
Arguments:
- features: bfloat16 [65536, 256], P(('dom', 'group')), may hold values from -6 to 6
- boundary: int32 [2048], P(('dom', 'group')), may hold values from 0 to 127, as said below
- request: int32 [128, 24], P(('dom', 'group')), may hold values from 0 to 63, as said below
- tile_slots: int32 [512, 8], P(('dom', 'group')), may hold values from 0 to 223, as said below
- neighbors: int32 [65536, 10], P(('dom', 'group')), may hold values from 0 to 127
- negatives: int32 [65536, 4], P(('dom', 'group')), may hold values from 0 to 127
- layer_weight: bfloat16 [512, 256], replicated, may hold values from -0.25 to 0.25
Outputs:
- feature_grad: float32 [65536, 256], P(('dom', 'group'))
- weight_grad: float32 [512, 256], replicated
- loss_mean: float32 [], replicated
Inputs may be any that keep to these rules, and one draw needn't show every extreme that they name: The 64 entries boundary[i * 64 to i * 64 + 63] are distinct numbers of device i's own row blocks. `request`: row i * 4 + e holds 24 distinct positions in the boundary list of device (i // 4) * 4 + e. `tile_slots`: entries are numbers s as in the first step; the 128 entries of one device are distinct and include every number from 128 to 223.
All inputs are finite; a program needn't handle non-finite values.
Results may differ from a plain program's by a relative error of at most 0.00075.
The roundings to bfloat16 on the way count: a program that leaves them out, or rounds other values in their place, can miss the bound.
Values may be sent and summed in bfloat16 or wider, within the bound.
No kernel may reach another device: no remote copies, remote signals or barrier semaphores. Data moves between devices by JAX's collectives and lax.ppermute only.
A program may use at most 64 MiB of HBM per device.

v0:
```python
import jax
import jax.numpy as jnp
from jax import lax
from jax.sharding import PartitionSpec as P

TILE = 128
BLK = 16
NBT = 8
DEG = 10
NNEG = 4
margin = 0.5
epsilon = 1e-06


def contract(form, left, right):
    return jnp.einsum(form, left, right, preferred_element_type=jnp.float32)


def tile_terms(own_rows, candidates, neighbor_ids, negative_ids, layer_weight):
    tile_count, tile_rows, feature_width = own_rows.shape
    cand_count = candidates.shape[1]
    degree = neighbor_ids.shape[-1]
    negative_count = negative_ids.shape[-1]
    slot_ids = jnp.arange(cand_count, dtype=jnp.int32)
    counts = jnp.sum((neighbor_ids[..., None] == slot_ids).astype(jnp.float32), axis=2).astype(
        jnp.bfloat16
    )
    aggregate = (contract("tuc,tcd->tud", counts, candidates) / degree).astype(jnp.bfloat16)
    joined = jnp.concatenate([own_rows, aggregate], axis=-1).reshape(-1, 2 * feature_width)
    preact = jnp.dot(joined, layer_weight, preferred_element_type=jnp.float32)
    gate_value = jax.nn.sigmoid(preact)
    hidden = preact * gate_value
    norm_scale = lax.rsqrt(jnp.mean(hidden * hidden, axis=-1, keepdims=True) + epsilon)
    embedding = hidden * norm_scale
    embed_half = embedding.astype(jnp.bfloat16).reshape(tile_count, tile_rows, feature_width)
    inv_root = feature_width ** (-0.5)
    scores = contract("tud,tcd->tuc", embed_half, candidates) * inv_root
    positive = (neighbor_ids[..., 0:1] == slot_ids).astype(jnp.float32)
    negative = (negative_ids[..., None] == slot_ids).astype(jnp.float32)
    pos_score = jnp.sum(scores * positive, axis=-1, keepdims=True)
    neg_score = jnp.sum(scores[:, :, None, :] * negative, axis=-1)
    excess = margin + neg_score - pos_score
    loss_sum = jnp.sum(jax.nn.softplus(excess)) / negative_count
    neg_weight = jax.nn.sigmoid(excess) / negative_count
    dscores = (
        jnp.sum(neg_weight[..., None] * negative, axis=2)
        - jnp.sum(neg_weight, axis=-1, keepdims=True) * positive
    ) * inv_root
    dscores_half = dscores.astype(jnp.bfloat16)
    dembedding = contract("tuc,tcd->tud", dscores_half, candidates).reshape(-1, feature_width)
    dcandidates = contract("tuc,tud->tcd", dscores_half, embed_half)
    dhidden = norm_scale * (
        dembedding - embedding * jnp.mean(dembedding * embedding, axis=-1, keepdims=True)
    )
    dpreact = (dhidden * gate_value * (1.0 + preact * (1.0 - gate_value))).astype(jnp.bfloat16)
    dweight = jnp.dot(joined.T, dpreact, preferred_element_type=jnp.float32)
    dinputs = jnp.dot(dpreact, layer_weight.T, preferred_element_type=jnp.float32)
    dself = dinputs[:, :feature_width].reshape(tile_count, tile_rows, feature_width)
    daggregate = (
        (dinputs[:, feature_width:] / degree)
        .astype(jnp.bfloat16)
        .reshape(tile_count, tile_rows, feature_width)
    )
    dcandidates = dcandidates + contract("tuc,tud->tcd", counts, daggregate)
    return (loss_sum, dweight, dself, dcandidates)


def per_device(features, boundary, request, tile_slots, neighbors, negatives, layer_weight):
    row_count, feature_width = features.shape
    peer_count = lax.axis_size("group")
    capacity = request.shape[1]
    bound_count = boundary.shape[0]
    block_count = row_count // BLK
    tile_count = tile_slots.shape[0]
    blocks = features.reshape(block_count, BLK, feature_width)
    shared = blocks[boundary].reshape(bound_count * BLK, feature_width)
    published = lax.all_gather(shared, "group", axis=0, tiled=True).reshape(
        peer_count, bound_count, BLK, feature_width
    )
    received = published[jnp.arange(peer_count, dtype=jnp.int32)[:, None], request]
    table_rows = jnp.concatenate(
        [blocks, received.reshape(peer_count * capacity, BLK, feature_width)], axis=0
    )
    slot_list = tile_slots.reshape(-1)
    candidates = table_rows[slot_list].reshape(tile_count, NBT * BLK, feature_width)
    own_rows = features.reshape(tile_count, TILE, feature_width)
    neighbor_ids = neighbors.reshape(tile_count, TILE, DEG)
    negative_ids = negatives.reshape(tile_count, TILE, NNEG)
    loss_sum, dweight, dself, dcandidates = tile_terms(
        own_rows, candidates, neighbor_ids, negative_ids, layer_weight
    )
    table_grad = jnp.zeros((block_count + peer_count * capacity, BLK, feature_width), jnp.float32)
    table_grad = table_grad.at[slot_list].add(dcandidates.reshape(-1, BLK, feature_width))
    own_grad = table_grad[:block_count] + dself.reshape(block_count, BLK, feature_width)
    incoming = table_grad[block_count:]
    sectioned = jnp.zeros((peer_count, bound_count, BLK, feature_width), jnp.float32)
    sectioned = sectioned.at[jnp.arange(peer_count, dtype=jnp.int32)[:, None], request].add(
        incoming.reshape(peer_count, capacity, BLK, feature_width)
    )
    summed_back = lax.psum_scatter(
        sectioned.reshape(peer_count * bound_count * BLK, feature_width),
        "group",
        scatter_dimension=0,
        tiled=True,
    )
    own_grad = own_grad.at[boundary].add(summed_back.reshape(bound_count, BLK, feature_width))
    totals = lax.psum((dweight, loss_sum), ("dom", "group"))
    device_total = lax.axis_size(("dom", "group"))
    return (
        own_grad.reshape(row_count, feature_width),
        totals[0] / row_count,
        totals[1] / (row_count * device_total),
    )


def solution(mesh):
    return jax.shard_map(
        per_device,
        mesh=mesh,
        in_specs=(
            P(("dom", "group"), None),
            P(("dom", "group")),
            P(("dom", "group"), None),
            P(("dom", "group"), None),
            P(("dom", "group"), None),
            P(("dom", "group"), None),
            P(),
        ),
        out_specs=(P(("dom", "group"), None), P(), P()),
        check_vma=False,
    )
```

profile of v0, /device:TPU:0, one launch (start us, length us, event | category | flops | bytes accessed | tf_op | source)
XLA Modules:
  0.0 263.6 jit_solution(1300090860702294701)
XLA Ops:
  7.9 2.7 %gather_fusion = bf16[64,16,256]{2,1,0:T(8,128)(2,1)} fusion(bf16[128,16,256]{2,1,0:T(8,128)(2,1)} %bitcast.70, s32[1024]{0:T(1024)S(1)} %pad_clamp_fusion.1), kind=kCustom, calls=%fused_computation | custom fusion | bytes 1048832 | tf_op jit(solution)/shard_map/gather | solution.py:76
  13.4 4.0 %convert_reduce_fusion = bf16[16,128,128]{2,1,0:T(8,128)(2,1)S(1)} fusion(s32[16,128,10]{1,2,0:T(8,128)S(1)} %copy.24), kind=kLoop, calls=%fused_computation.6 | loop fusion | flops 7602176 | bytes 606208 | tf_op jit(solution)/shard_map/reduce_sum | solution.py:25
  17.5 18.7 %all-gather.2.cloned.1.call-done = bf16[4096,256]{1,0:T(8,128)(2,1)} async-done(((bf16[1024,256]{1,0:T(8,128)(2,1)}), bf16[4096,256]{1,0:T(8,128)(2,1)}) %all-gather.2.cloned.1.call-update) | async-done | bytes 2097168 | tf_op jit(solution)/shard_map/all_gather | solution.py:77
  36.2 2.6 gather_fusion.1
  38.8 1.4 pad_maximum_fusion.1
  40.2 2.1 gather_fusion.2
  43.5 1.1 multiply_reduce_fusion
  45.3 1.0 copy-done.5
  46.3 1.4 select_reduce_fusion.2
  47.7 2.5 copy.25
  50.3 3.9 %select_reduce_fusion.1 = f32[16,128,4]{1,2,0:T(4,128)S(1)} fusion(f32[16,128,128]{2,1,0:T(8,128)} %copy.25, s32[16,128,4]{1,2,0:T(4,128)S(1)} %bitcast.78), kind=kLoop, calls=%fused_computation.9 | loop fusion | flops 3137536 | bytes 1114112 | tf_op jit(solution)/shard_map/reduce_sum | solution.py:41
  54.8 3.8 %select_reduce_fusion = f32[16,128,128]{2,1,0:T(8,128)} fusion(f32[16,128,4]{1,2,0:T(4,128)S(1)} %get-tuple-element.4, s32[16,128,4]{1,2,0:T(4,128)S(1)} %bitcast.79), kind=kLoop, calls=%fused_computation.8 | loop fusion | flops 2883584 | bytes 1114112 | tf_op jit(solution)/shard_map/reduce_sum | solution.py:46
  58.6 2.5 copy.27
  61.1 1.9 fusion.12
  63.0 1.7 fusion.13
  64.7 1.0 fusion.1
  65.8 1.4 fusion.5
  67.3 1.5 fusion.7
  68.8 2.7 %fusion.27 = f32[2048,512]{1,0:T(8,128)} fusion(bf16[2048,256]{1,0:T(8,128)(2,1)S(1)} %fusion.5, bf16[512,256]{1,0:T(8,128)(2,1)S(1)} %copy-done), kind=kOutput, calls=%fused_computation.70 | convolution fusion | flops 536870912 | bytes 5505024 | tf_op jit(solution)/shard_map/dot_general | solution.py:57
  71.8 2.7 %fusion = (bf16[2048,256]{1,0:T(8,128)(2,1)S(1)}, f32[2048,256]{1,0:T(8,128)S(1)}) fusion(f32[2048,512]{1,0:T(8,128)} %fusion.27), kind=kLoop, calls=%fused_computation.13 | loop fusion | flops 1048576 | bytes 7340032 | tf_op jit(solution)/shard_map/convert_element_type | solution.py:61
  74.7 1.8 convolution_add_fusion
  76.5 2.3 broadcast_in_dim.10
  78.8 17.5 %scatter_fusion = f32[224,16,256]{2,1,0:T(8,128)} fusion(f32[224,16,256]{2,1,0:T(8,128)} %broadcast_in_dim.10, s32[128]{0:T(128)S(1)} %fusion.19, f32[128,16,256]{2,1,0:T(8,128)} %bitcast.65), kind=kCustom, calls=%fused_computation.3 | custom fusion | flops 524288 | bytes 6291968 | tf_op jit(solution)/shard_map/scatter-add | solution.py:93
  96.2 2.7 %slice.32 = f32[96,16,256]{2,1,0:T(8,128)} slice(f32[224,16,256]{2,1,0:T(8,128)} %scatter_fusion), slice={[128:224], [0:16], [0:256]} | slice | bytes 3145728 | tf_op jit(solution)/shard_map/slice | solution.py:95
  98.9 2.5 broadcast_in_dim.14
  101.3 14.0 %scatter_fusion.1 = f32[4,64,16,256]{3,2,1,0:T(8,128)} fusion(f32[4,64,16,256]{3,2,1,0:T(8,128)} %broadcast_in_dim.14, s32[96]{0:T(128)S(1)} %reshape.154, f32[96,16,256]{2,1,0:T(8,128)} %slice.32), kind=kCustom, calls=%fused_computation.4 | custom fusion | flops 393216 | bytes 4719360 | tf_op jit(solution)/shard_map/scatter-add | solution.py:97
  116.0 39.3 %psum.15 = f32[]{:T(128)} all-reduce(f32[]{:T(128)S(6)} %div.58), channel_id=1, replica_groups=mesh['dom'=8,'group'=4] {'dom','group'}, use_global_device_ids=true, to_apply=%region_13.14 | all-reduce | flops 1 | bytes 8 | tf_op jit(solution)/shard_map/psum | solution.py:107
  156.0 3.4 %slice_add_fusion = f32[128,16,256]{2,1,0:T(8,128)} fusion(f32[128,16,256]{2,1,0:T(8,128)S(1)} %bitcast.64, f32[224,16,256]{2,1,0:T(8,128)} %scatter_fusion), kind=kLoop, calls=%fused_computation.11 | loop fusion | flops 524288 | bytes 6291456 | tf_op jit(solution)/shard_map/add | solution.py:94
  159.4 41.4 %all-reduce.2.cloned.1.call-done = f32[512,256]{1,0:T(8,128)} async-done(((f32[512,256]{1,0:T(8,128)}), f32[512,256]{1,0:T(8,128)}) %all-reduce.2.cloned.1.call-update) | async-done | bytes 524304 | tf_op jit(solution)/shard_map/psum | solution.py:107
  200.8 1.9 broadcast_multiply_fusion
  202.7 44.3 %reduce-scatter.2.cloned.1.call-done = f32[1024,256]{1,0:T(8,128)} async-done(((f32[4096,256]{1,0:T(8,128)}), f32[1024,256]{1,0:T(8,128)}) %reduce-scatter.2.cloned.1.call-update) | async-done | bytes 1048592 | tf_op jit(solution)/shard_map/reduce_scatter | solution.py:100
  247.0 9.0 %scatter_fusion.2 = f32[128,16,256]{2,1,0:T(8,128)} fusion(f32[128,16,256]{2,1,0:T(8,128)} %slice_add_fusion, s32[64]{0:T(128)S(1)} %compare_select_fusion.2, f32[64,16,256]{2,1,0:T(8,128)} %bitcast.75), kind=kCustom, calls=%fused_computation.5 | custom fusion | flops 262144 | bytes 3145984 | tf_op jit(solution)/shard_map/scatter-add | solution.py:106
  (49 shorter events, 6.5 us)
Async XLA Ops:
  7.2 35.6 %copy-start = (bf16[512,256]{1,0:T(8,128)(2,1)S(1)}, bf16[512,256]{1,0:T(8,128)(2,1)}, u32[]{:S(2)}) copy-start(bf16[512,256]{1,0:T(8,128)(2,1)} %param.13) | copy-start | bytes 786436
  7.2 29.0 %all-gather.2.cloned.1.call-start = ((), (), s32[]{:S(2)}) async-start(), calls=%async_computation.1 | async-start | bytes 2621440 | tf_op jit(solution)/shard_map/all_gather | solution.py:77
  7.9 30.8 %copy-start.7 = (bf16[2048,256]{1,0:T(8,128)(2,1)S(1)}, bf16[2048,256]{1,0:T(8,128)(2,1)}, u32[]{:S(2)}) copy-start(bf16[2048,256]{1,0:T(8,128)(2,1)} %param.7) | copy-start | bytes 3145732
  10.7 190.2 %all-reduce.2.cloned.1.call-start = ((), (), s32[]{:S(2)}) async-start(), calls=%async_computation.3 | async-start | bytes 1048576 | tf_op jit(solution)/shard_map/psum | solution.py:107
  17.5 24.9 %copy-start.3 = (bf16[16,128,128]{2,1,0:T(8,128)(2,1)}, bf16[16,128,128]{2,1,0:T(8,128)(2,1)S(1)}, u32[]{:S(2)}) copy-start(bf16[16,128,128]{2,1,0:T(8,128)(2,1)S(1)} %convert_reduce_fusion) | copy-start | bytes 1572868
  42.3 1.2 copy-start.8
  42.8 1.9 copy-start.10
  45.3 1.0 copy-start.5
  46.3 4.0 %copy-start.12 = (s32[2048,4]{0,1:T(4,128)S(1)}, s32[2048,4]{0,1:T(4,128)}, u32[]{:S(2)}) copy-start(s32[2048,4]{0,1:T(4,128)} %param.12) | copy-start | bytes 98308
  61.1 1.9 copy-start.1
  61.1 1.9 copy-start.6
  65.7 1.5 copy-start.9
  65.8 1.5 copy-start.11
  71.5 3.0 %copy-start.4 = (bf16[16,128,128]{2,1,0:T(8,128)(2,1)S(1)}, bf16[16,128,128]{2,1,0:T(8,128)(2,1)}, u32[]{:S(2)}) copy-start(bf16[16,128,128]{2,1,0:T(8,128)(2,1)} %copy-done.3) | copy-start | bytes 1572868
  71.5 175.4 %reduce-scatter.2.cloned.1.call-start = ((), (), s32[]{:S(2)}) async-start(), calls=%async_computation.2 | async-start | bytes 5242880 | tf_op jit(solution)/shard_map/reduce_scatter | solution.py:100
  71.8 2.9 %copy-start.2 = (f32[16,128,256]{2,1,0:T(8,128)S(1)}, f32[16,128,256]{2,1,0:T(8,128)}, u32[]{:S(2)}) copy-start(f32[16,128,256]{2,1,0:T(8,128)} %fusion.13) | copy-start | bytes 6291460
Sparse Core Ops, SparseCore 0:
  10.8 25.3 all-gather.1
  71.6 129.1 all-reduce.1
  203.3 43.5 reduce-scatter.1
where the time goes:
time: 265 us; the launch traced here: 264 us
  waiting for transfers between devices  104 us (39%)
  other arithmetic  66.5 us (25%)
  blocking collectives  39.3 us (15%)
  local copies, waits for them, and re-layouts  24 us (9%)
  between operations  16.5 us (6%)
  matrix products  12.6 us (5%)
    reduce_scatter x1, waiting for transfers between devices, per_device(): lax.psum_scatter(sectioned.reshape(peer_count * bound_count * BLK, featur...  44.3 us
    psum x1, waiting for transfers between devices, per_device(): totals = lax.psum((dweight, loss_sum), ('dom', 'group'))  41.4 us
    psum x1, blocking collectives, per_device(): totals = lax.psum((dweight, loss_sum), ('dom', 'group'))  39.3 us
    all_gather x1, waiting for transfers between devices, per_device(): lax.all_gather(shared, 'group', axis=0, tiled=True)  18.7 us
    scatter-add x1, other arithmetic, per_device(): table_grad.at[slot_list].add(dcandidates.reshape(-1, BLK, feature_width))  17.5 us
    scatter-add x1, other arithmetic, per_device(): sectioned.at[jnp.arange(peer_count, dtype=jnp.int32)[:, None], request]  14 us
    scatter-add x1, other arithmetic, per_device(): own_grad.at[boundary]  9 us
    dot_general x5, matrix products, contract(): return jnp.einsum(form, left, right, preferred_element_type=jnp.float32)  7.26 us
  transfers between devices with their start and end apart: 3, of which 3 were waited for; matrix products, arithmetic and copies ran while one was open for 21% of the time, Pallas kernels for 0%

commit v1 on v0

--- a/solution.py
+++ b/solution.py
@@ -10,6 +10,19 @@
 NNEG = 4
 margin = 0.5
 epsilon = 1e-06
+
+
+def gather_around(shard, axis, dim):
+    size, index, extent = (lax.axis_size(axis), lax.axis_index(axis), shard.shape[dim])
+    right = [(i, (i + 1) % size) for i in range(size)]
+    filled = jnp.zeros((*shard.shape[:dim], size * extent, *shard.shape[dim + 1 :]), shard.dtype)
+    block = shard
+    for step in range(size):
+        source = (index - step) % size
+        filled = lax.dynamic_update_slice_in_dim(filled, block, source * extent, axis=dim)
+        if step < size - 1:
+            block = lax.ppermute(block, axis, right)
+    return filled
 
 
 def contract(form, left, right):
@@ -74,7 +87,7 @@
     tile_count = tile_slots.shape[0]
     blocks = features.reshape(block_count, BLK, feature_width)
     shared = blocks[boundary].reshape(bound_count * BLK, feature_width)
-    published = lax.all_gather(shared, "group", axis=0, tiled=True).reshape(
+    published = gather_around(shared, "group", 0).reshape(
         peer_count, bound_count, BLK, feature_width
     )
     received = published[jnp.arange(peer_count, dtype=jnp.int32)[:, None], request]

time: 265 us -> 242 us (0.913)
  waiting for transfers between devices: 104 us -> 72.8 us
    reduce_scatter x1, waiting for transfers between devices: 44.3 us -> 0.01 us  [per_device(): lax.psum_scatter(sectioned.reshape(peer_count * bound_count * BLK, featur...]
    all_gather x1 -> x0, waiting for transfers between devices: 18.7 us -> none  [per_device(): lax.all_gather(shared, 'group', axis=0, tiled=True)]
    ppermute x0 -> x3, waiting for transfers between devices: none -> 17 us  [gather_around(): block = lax.ppermute(block, axis, right)]
    psum x1, waiting for transfers between devices: 41.4 us -> 55.8 us  [per_device(): totals = lax.psum((dweight, loss_sum), ('dom', 'group'))]
    dynamic_update_slice x0 -> x4, local copies, waits for them, and re-layouts: none -> 3.47 us  [gather_around(): lax.dynamic_update_slice_in_dim(filled, block, source * extent, axis=dim)]
  transfers between devices with their start and end apart: 3 -> 5, of which waited for: 3 -> 4; matrix products, arithmetic and copies ran while one was open for 21% -> 24% of each run, Pallas kernels for 0% -> 0%
where the time goes in v1:
time: 242 us; the launch traced here: 240 us
  waiting for transfers between devices  72.8 us (30%)
  other arithmetic  67.9 us (28%)
  blocking collectives  41.8 us (17%)
  local copies, waits for them, and re-layouts  26.2 us (11%)
  between operations  18.3 us (8%)
  matrix products  12.6 us (5%)
    psum x1, waiting for transfers between devices, per_device(): totals = lax.psum((dweight, loss_sum), ('dom', 'group'))  55.8 us
    psum x1, blocking collectives, per_device(): totals = lax.psum((dweight, loss_sum), ('dom', 'group'))  41.8 us
    scatter-add x1, other arithmetic, per_device(): table_grad.at[slot_list].add(dcandidates.reshape(-1, BLK, feature_width))  17.5 us
    ppermute x3, waiting for transfers between devices, gather_around(): block = lax.ppermute(block, axis, right)  17 us
    scatter-add x1, other arithmetic, per_device(): sectioned.at[jnp.arange(peer_count, dtype=jnp.int32)[:, None], request]  14 us
    scatter-add x1, other arithmetic, per_device(): own_grad.at[boundary]  9 us
    dot_general x5, matrix products, contract(): return jnp.einsum(form, left, right, preferred_element_type=jnp.float32)  7.26 us
  transfers between devices with their start and end apart: 5, of which 4 were waited for; matrix products, arithmetic and copies ran while one was open for 24% of the time, Pallas kernels for 0%

profile of v1, /device:TPU:0, one launch (start us, length us, event | category | flops | bytes accessed | tf_op | source)
XLA Modules:
  0.0 240.4 jit_solution(17279074850848594796)
XLA Ops:
  8.8 1.8 gather_fusion
  13.6 6.3 %collective-permute-done = bf16[1024,256]{1,0:T(8,128)(2,1)S(1)} collective-permute-done((bf16[1024,256]{1,0:T(8,128)(2,1)S(1)}, bf16[1024,256]{1,0:T(8,128)(2,1)S(1)}, u32[]{:S(2)}, u32[]{:S(2)}) %collective-permute-start) | collective-permute-done | bytes 524320 | tf_op jit(solution)/shard_map/ppermute | solution.py:24
  20.2 8.5 %collective-permute-done.1 = bf16[1024,256]{1,0:T(8,128)(2,1)} collective-permute-done((bf16[1024,256]{1,0:T(8,128)(2,1)S(1)}, bf16[1024,256]{1,0:T(8,128)(2,1)}, u32[]{:S(2)}, u32[]{:S(2)}) %collective-permute-start.1) | collective-permute-done | bytes 524320 | tf_op jit(solution)/shard_map/ppermute | solution.py:24
  28.9 4.0 %convert_reduce_fusion = bf16[16,128,128]{2,1,0:T(8,128)(2,1)S(1)} fusion(s32[16,128,10]{1,2,0:T(8,128)S(1)} %copy.24), kind=kLoop, calls=%fused_computation.6 | loop fusion | flops 7602176 | bytes 606208 | tf_op jit(solution)/shard_map/reduce_sum | solution.py:38
  33.0 1.3 constant_dynamic-update-slice_fusion.2
  35.3 2.2 collective-permute-done.2
  38.7 2.0 gather_fusion.1
  40.7 2.9 %pad_maximum_fusion.1 = bf16[224,16,256]{2,1,0:T(8,128)(2,1)} fusion(bf16[96,16,256]{2,1,0:T(8,128)(2,1)} %gather_fusion.1, bf16[128,16,256]{2,1,0:T(8,128)(2,1)} %bitcast.72), kind=kLoop, calls=%fused_computation.27 | loop fusion | flops 917504 | bytes 3670016 | tf_op jit(solution)/shard_map/concatenate | solution.py:94
  43.5 2.1 gather_fusion.2
  46.9 1.1 multiply_reduce_fusion
  49.7 1.4 select_reduce_fusion.2
  51.1 2.5 %copy.25 = f32[16,128,128]{2,1,0:T(8,128)} copy(f32[16,128,128]{1,2,0:T(8,128)} %get-tuple-element.13) | data formatting | bytes 2097152 | tf_op jit(solution)/shard_map/mul | solution.py:50
  53.6 3.9 %select_reduce_fusion.1 = f32[16,128,4]{1,2,0:T(4,128)S(1)} fusion(f32[16,128,128]{2,1,0:T(8,128)} %copy.25, s32[16,128,4]{1,2,0:T(4,128)S(1)} %bitcast.79), kind=kLoop, calls=%fused_computation.9 | loop fusion | flops 3137536 | bytes 1114112 | tf_op jit(solution)/shard_map/reduce_sum | solution.py:54
  58.2 3.8 %select_reduce_fusion = f32[16,128,128]{2,1,0:T(8,128)} fusion(f32[16,128,4]{1,2,0:T(4,128)S(1)} %get-tuple-element.4, s32[16,128,4]{1,2,0:T(4,128)S(1)} %bitcast.80), kind=kLoop, calls=%fused_computation.8 | loop fusion | flops 2883584 | bytes 1114112 | tf_op jit(solution)/shard_map/reduce_sum | solution.py:59
  61.9 2.5 %copy.27 = f32[16,128,128]{1,2,0:T(8,128)} copy(f32[16,128,128]{2,1,0:T(8,128)} %select_reduce_fusion) | data formatting | bytes 2097152 | tf_op jit(solution)/shard_map/reduce_sum | solution.py:59
  64.5 1.9 fusion.12
  66.4 1.7 fusion.13
  69.1 1.4 fusion.5
  70.7 1.5 fusion.7
  72.2 2.7 %fusion.27 = f32[2048,512]{1,0:T(8,128)} fusion(bf16[2048,256]{1,0:T(8,128)(2,1)S(1)} %fusion.5, bf16[512,256]{1,0:T(8,128)(2,1)S(1)} %copy-done), kind=kOutput, calls=%fused_computation.74 | convolution fusion | flops 536870912 | bytes 5505024 | tf_op jit(solution)/shard_map/dot_general | solution.py:70
  75.2 2.7 %fusion = (bf16[2048,256]{1,0:T(8,128)(2,1)S(1)}, f32[2048,256]{1,0:T(8,128)S(1)}) fusion(f32[2048,512]{1,0:T(8,128)} %fusion.27), kind=kLoop, calls=%fused_computation.13 | loop fusion | flops 1048576 | bytes 7340032 | tf_op jit(solution)/shard_map/convert_element_type | solution.py:74
  78.0 1.8 convolution_add_fusion
  79.8 2.3 broadcast_in_dim.12
  82.1 17.5 %scatter_fusion = f32[224,16,256]{2,1,0:T(8,128)} fusion(f32[224,16,256]{2,1,0:T(8,128)} %broadcast_in_dim.12, s32[128]{0:T(128)S(1)} %fusion.19, f32[128,16,256]{2,1,0:T(8,128)} %bitcast.65), kind=kCustom, calls=%fused_computation.3 | custom fusion | flops 524288 | bytes 6291968 | tf_op jit(solution)/shard_map/scatter-add | solution.py:106
  99.6 2.7 %slice.32 = f32[96,16,256]{2,1,0:T(8,128)} slice(f32[224,16,256]{2,1,0:T(8,128)} %scatter_fusion), slice={[128:224], [0:16], [0:256]} | slice | bytes 3145728 | tf_op jit(solution)/shard_map/slice | solution.py:108
  102.3 2.5 %broadcast_in_dim.17 = f32[4,64,16,256]{3,2,1,0:T(8,128)} broadcast(f32[]{:T(128)} %constant.73.clone.1), dimensions={} | broadcast | bytes 4194308 | tf_op jit(solution)/shard_map/broadcast_in_dim | solution.py:109
  104.7 14.0 %scatter_fusion.1 = f32[4,64,16,256]{3,2,1,0:T(8,128)} fusion(f32[4,64,16,256]{3,2,1,0:T(8,128)} %broadcast_in_dim.17, s32[96]{0:T(128)S(1)} %reshape.154, f32[96,16,256]{2,1,0:T(8,128)} %slice.32), kind=kCustom, calls=%fused_computation.4 | custom fusion | flops 393216 | bytes 4719360 | tf_op jit(solution)/shard_map/scatter-add | solution.py:110
  119.4 41.8 %psum.15 = f32[]{:T(128)} all-reduce(f32[]{:T(128)S(6)} %div.58), channel_id=1, replica_groups=mesh['dom'=8,'group'=4] {'dom','group'}, use_global_device_ids=true, to_apply=%region_13.14 | all-reduce | flops 1 | bytes 8 | tf_op jit(solution)/shard_map/psum | solution.py:120
  161.8 3.4 %slice_add_fusion = f32[128,16,256]{2,1,0:T(8,128)} fusion(f32[128,16,256]{2,1,0:T(8,128)S(1)} %bitcast.64, f32[224,16,256]{2,1,0:T(8,128)} %scatter_fusion), kind=kLoop, calls=%fused_computation.11 | loop fusion | flops 524288 | bytes 6291456 | tf_op jit(solution)/shard_map/add | solution.py:107
  165.2 55.8 %all-reduce.2.cloned.1.call-done = f32[512,256]{1,0:T(8,128)} async-done(((f32[512,256]{1,0:T(8,128)}), f32[512,256]{1,0:T(8,128)}) %all-reduce.2.cloned.1.call-update) | async-done | bytes 524304 | tf_op jit(solution)/shard_map/psum | solution.py:120
  221.0 1.9 broadcast_multiply_fusion
  222.9 9.0 %scatter_fusion.2 = f32[128,16,256]{2,1,0:T(8,128)} fusion(f32[128,16,256]{2,1,0:T(8,128)} %slice_add_fusion, s32[64]{0:T(128)S(1)} %compare_select_fusion.2, f32[64,16,256]{2,1,0:T(8,128)} %bitcast.77), kind=kCustom, calls=%fused_computation.5 | custom fusion | flops 262144 | bytes 3145984 | tf_op jit(solution)/shard_map/scatter-add | solution.py:119
  (57 shorter events, 11.3 us)
Async XLA Ops:
  8.0 38.2 %copy-start = (bf16[512,256]{1,0:T(8,128)(2,1)S(1)}, bf16[512,256]{1,0:T(8,128)(2,1)}, u32[]{:S(2)}) copy-start(bf16[512,256]{1,0:T(8,128)(2,1)} %param.13) | copy-start | bytes 786436
  8.0 213.0 %all-reduce.2.cloned.1.call-start = ((), (), s32[]{:S(2)}) async-start(), calls=%async_computation.2 | async-start | bytes 1048576 | tf_op jit(solution)/shard_map/psum | solution.py:120
  10.6 9.4 %collective-permute-start = (bf16[1024,256]{1,0:T(8,128)(2,1)S(1)}, bf16[1024,256]{1,0:T(8,128)(2,1)S(1)}, u32[]{:S(2)}, u32[]{:S(2)}) collective-permute-start(bf16[1024,256]{1,0:T(8,128)(2,1)S(1)} %bitcast.73), channel_id=1, source_target_pairs={{0,1},{1,2},{2,3},{3,0},{4,5},{5,6},{6,7},{7,4},{8,9},{9,10},{10,1... | collective-permute-start | bytes 1572872 | tf_op jit(solution)/shard_map/ppermute | solution.py:24
  19.9 8.8 %copy-start.11 = (bf16[1024,256]{1,0:T(8,128)(2,1)}, bf16[1024,256]{1,0:T(8,128)(2,1)S(1)}, u32[]{:S(2)}) copy-start(bf16[1024,256]{1,0:T(8,128)(2,1)S(1)} %collective-permute-done) | copy-start | bytes 1572868
  19.9 8.7 %collective-permute-start.1 = (bf16[1024,256]{1,0:T(8,128)(2,1)S(1)}, bf16[1024,256]{1,0:T(8,128)(2,1)}, u32[]{:S(2)}, u32[]{:S(2)}) collective-permute-start(bf16[1024,256]{1,0:T(8,128)(2,1)S(1)} %collective-permute-done), channel_id=1, source_target_pairs={{0,1},{1,2},{2,3},{3,0},{4,5},{5,6},{6,7},{7,4},{8,9},{9,10},{10,1... | collective-permute-start | bytes 1572872 | tf_op jit(solution)/shard_map/ppermute | solution.py:24
  28.7 8.9 %collective-permute-start.2 = (bf16[1024,256]{1,0:T(8,128)(2,1)}, bf16[1024,256]{1,0:T(8,128)(2,1)}, u32[]{:S(2)}, u32[]{:S(2)}) collective-permute-start(bf16[1024,256]{1,0:T(8,128)(2,1)} %collective-permute-done.1), channel_id=1, source_target_pairs={{0,1},{1,2},{2,3},{3,0},{4,5},{5,6},{6,7},{7,4},{8,9},{9,10},{10,1... | collective-permute-start | bytes 1572872 | tf_op jit(solution)/shard_map/ppermute | solution.py:24
  33.0 12.7 %copy-start.3 = (bf16[16,128,128]{2,1,0:T(8,128)(2,1)}, bf16[16,128,128]{2,1,0:T(8,128)(2,1)S(1)}, u32[]{:S(2)}) copy-start(bf16[16,128,128]{2,1,0:T(8,128)(2,1)S(1)} %convert_reduce_fusion) | copy-start | bytes 1572868
  45.7 1.2 copy-start.7
  46.1 1.9 copy-start.9
  48.6 1.0 copy-start.5
  49.7 4.0 %copy-start.12 = (s32[2048,4]{0,1:T(4,128)S(1)}, s32[2048,4]{0,1:T(4,128)}, u32[]{:S(2)}) copy-start(s32[2048,4]{0,1:T(4,128)} %param.12) | copy-start | bytes 98308
  64.5 1.9 copy-start.1
  64.5 1.9 copy-start.6
  69.1 1.5 copy-start.8
  69.1 1.5 copy-start.10
  74.9 3.0 %copy-start.4 = (bf16[16,128,128]{2,1,0:T(8,128)(2,1)S(1)}, bf16[16,128,128]{2,1,0:T(8,128)(2,1)}, u32[]{:S(2)}) copy-start(bf16[16,128,128]{2,1,0:T(8,128)(2,1)} %copy-done.3) | copy-start | bytes 1572868
  74.9 147.9 %reduce-scatter.2.cloned.1.call-start = ((), (), s32[]{:S(2)}) async-start(), calls=%async_computation.1 | async-start | bytes 5242880 | tf_op jit(solution)/shard_map/reduce_scatter | solution.py:113
  75.1 2.9 %copy-start.2 = (f32[16,128,256]{2,1,0:T(8,128)S(1)}, f32[16,128,256]{2,1,0:T(8,128)}, u32[]{:S(2)}) copy-start(f32[16,128,256]{2,1,0:T(8,128)} %fusion.13) | copy-start | bytes 6291460
Sparse Core Ops, SparseCore 0:
  75.0 145.9 all-reduce.1
Sparse Core Ops, SparseCore 1:
  118.8 47.2 reduce-scatter.1
